TPU v7x, 32 devices: a whole 2x2x4 slice. The times are simulated.
32 devices in a mesh: grp: 2 (over core), dp: 4 (over y, x), sp: 4 (over z).
Axes of the slice: x: 2, y: 2, z: 4, core: 2. Of those that a mesh axis runs over, the one named last changes fastest.
Arguments:
- vis: bfloat16 [512, 5120], P(('grp', 'dp', 'sp')), may hold values from -6 to 6
- merge_weight: bfloat16 [5120, 8192], P('dp', ('grp', 'sp')), may hold values from -0.078125 to 0.078125
- img_counts: int32 [32], P('dp'), may hold values from 1 to 16
- img_pos: int32 [512], P(('grp', 'dp', 'sp')), may hold values from 0 to 127, as said below
- text: bfloat16 [4096, 8192], P(('grp', 'dp', 'sp')), may hold values from -6 to 6
- cot: bfloat16 [4096, 8192], P(('grp', 'dp', 'sp')), may hold values from -6 to 6
- gain: float32 [8192], replicated, may hold values from 0.25 to 1.75
Outputs:
- vis_grad: bfloat16 [512, 5120], P(('grp', 'dp', 'sp'))
- gain_grad: float32 [8192], replicated
Inputs may be any that keep to these rules, and one draw needn't show every extreme that they name: `img_pos`: within one device's block the 16 positions are distinct. `img_counts`: the counts of one image group sum to at most 128.
All inputs are finite; a program needn't handle non-finite values.
Results may differ from a plain program's by a relative error of at most 0.014.
Values may be sent and summed in bfloat16 or wider, within the bound.
No kernel may reach another device: no remote copies, remote signals or barrier semaphores. Data moves between devices by JAX's collectives and lax.ppermute only.
A program may use at most 128 MiB of HBM per device.

v0:
```python
import jax
import jax.numpy as jnp
from jax import lax
from jax.sharding import PartitionSpec as P


def body(vis, merge_weight, img_counts, img_pos, text, cot, gain):
    rows_dev = vis.shape[0]
    tok_rows = text.shape[0]
    group_vis = lax.all_gather(vis, ("grp", "sp"), axis=0, tiled=True)
    full_weight = lax.all_gather(merge_weight, "dp", axis=0, tiled=True)
    partial_value = jnp.dot(group_vis, full_weight, preferred_element_type=jnp.float32)
    emb = lax.all_to_all(
        partial_value.astype(jnp.bfloat16), ("grp", "sp"), split_axis=0, concat_axis=1, tiled=True
    )
    total_live = jnp.sum(img_counts)
    member = lax.axis_index("grp") * lax.axis_size("sp") + lax.axis_index("sp")
    group_row = member * rows_dev + jnp.arange(rows_dev, dtype=jnp.int32)
    live = group_row < total_live
    places = jnp.arange(tok_rows, dtype=jnp.int32)
    select = (img_pos[None, :] == places[:, None]) & live[None, :]
    taken = jnp.any(select, axis=1)
    select_b = select.astype(jnp.bfloat16)
    placed = jnp.dot(select_b, emb, preferred_element_type=jnp.float32)
    hidden = jnp.where(taken[:, None], placed, text.astype(jnp.float32))
    rinv = lax.rsqrt(jnp.mean(hidden * hidden, axis=1, keepdims=True) + 1e-06)
    cotf = cot.astype(jnp.float32)
    part_gain = jnp.sum(cotf * hidden * rinv, axis=0)
    scaled = cotf * gain[None, :]
    inner = jnp.mean(scaled * hidden, axis=1, keepdims=True)
    dhid = (rinv * scaled - hidden * rinv**3 * inner).astype(jnp.bfloat16)
    demb = jnp.dot(select_b.T, dhid, preferred_element_type=jnp.float32)
    demb = jnp.where(live[:, None], demb, 0.0).astype(jnp.bfloat16)
    returned = lax.all_to_all(demb, ("grp", "sp"), split_axis=1, concat_axis=0, tiled=True)
    terms = lax.dot_general(
        returned, full_weight, (((1,), (1,)), ((), ())), preferred_element_type=jnp.float32
    )
    vis_grad = lax.psum_scatter(
        terms.astype(jnp.bfloat16), ("grp", "sp"), scatter_dimension=0, tiled=True
    )
    gain_grad = lax.psum(part_gain, ("grp", "dp", "sp"))
    return (vis_grad, gain_grad)


def solution(mesh):
    return jax.shard_map(
        body,
        mesh=mesh,
        in_specs=(
            P(("grp", "dp", "sp"), None),
            P("dp", ("grp", "sp")),
            P("dp"),
            P(("grp", "dp", "sp")),
            P(("grp", "dp", "sp"), None),
            P(("grp", "dp", "sp"), None),
            P(),
        ),
        out_specs=(P(("grp", "dp", "sp"), None), P()),
        check_vma=False,
    )
```

profile of v0, /device:TPU:0, one launch (start us, length us, event | category | flops | bytes accessed | tf_op | source)
XLA Modules:
  0.0 229.6 jit_solution(17347707635758896386)
XLA Ops:
  7.2 0.0 all-gather.3.cloned.1.call-start
  7.2 0.7 all-gather.3.cloned.1.call-update
  7.9 0.0 all-gather.5.cloned.1.call-start
  7.9 0.7 all-gather.5.cloned.1.call-update
  8.6 0.0 copy-start.4
  8.7 0.0 copy-start.3
  8.7 0.0 copy-start
  8.7 27.1 %all-gather.3.cloned.1.call-done = bf16[128,5120]{1,0:T(8,128)(2,1)} async-done(((bf16[16,5120]{1,0:T(8,128)(2,1)}), bf16[128,5120]{1,0:T(8,128)(2,1)}) %all-gather.3.cloned.1.call-update) | async-done | bytes 1310736 | tf_op jit(solution)/shard_map/all_gather | solution.py:10
  35.7 106.3 %all-gather.5.cloned.1.call-done = bf16[5120,1024]{1,0:T(8,128)(2,1)} async-done(((bf16[1280,1024]{1,0:T(8,128)(2,1)}), bf16[5120,1024]{1,0:T(8,128)(2,1)}) %all-gather.5.cloned.1.call-update) | async-done | bytes 10485776 | tf_op jit(solution)/shard_map/all_gather | solution.py:11
  142.1 6.6 %convolution_convert_fusion.1 = bf16[128,1024]{1,0:T(8,128)(2,1)} fusion(bf16[128,5120]{1,0:T(8,128)(2,1)} %all-gather.3.cloned.1.call-done, bf16[5120,1024]{1,0:T(8,128)(2,1)} %all-gather.5.cloned.1.call-done), kind=kOutput, calls=%fused_computation.14 | convolution fusion | flops 1342308352 | bytes 12058624 | tf_op jit(solution)/shard_map/dot_general | solution.py:12
  148.7 4.7 %all-to-all-start = ((bf16[8,16,1024]{2,1,0:T(8,128)(2,1)}), bf16[8,16,1024]{2,1,0:T(8,128)(2,1)S(1)}, u32[]{:S(2)}, u32[]{:S(2)}) async-start(bf16[8,16,1024]{2,1,0:T(8,128)(2,1)} %bitcast), calls=%async_computation | async-start | bytes 524288 | tf_op jit(solution)/shard_map/all_to_all | solution.py:13
  153.4 0.0 reduce-scatter.2.cloned.1.call-start
  153.5 0.0 copy-done.4
  153.5 0.6 reduce_sum.36
  154.1 0.7 add_compare_fusion
  154.8 0.0 copy-done.3
  154.8 0.1 fusion.12
  154.9 7.9 %all-to-all-done = bf16[8,16,1024]{2,1,0:T(8,128)(2,1)S(1)} async-done(((bf16[8,16,1024]{2,1,0:T(8,128)(2,1)}), bf16[8,16,1024]{2,1,0:T(8,128)(2,1)S(1)}, u32[]{:S(2)}, u32[]{:S(2)}) %all-to-all-start) | async-done | bytes 262176 | tf_op jit(solution)/shard_map/all_to_all | solution.py:13
  162.8 0.0 copy-done
  162.8 0.0 slice-start
  162.8 1.0 multiply_reduce_fusion
  163.8 0.0 copy-done.2
  163.8 0.6 copy-done.1
  164.4 1.5 fusion.7
  165.9 1.1 fusion
  167.1 11.8 %all_to_all.38 = bf16[16,8,1024]{2,0,1:T(8,128)(2,1)S(1)} all-to-all(bf16[16,8,1024]{2,0,1:T(8,128)(2,1)S(1)} %bitcast.21), channel_id=1, replica_groups=mesh['grp'=2,'dp'=4,'sp'=4] {'grp','sp'}, dimensions={1} | all-to-all | bytes 524288 | tf_op jit(solution)/shard_map/all_to_all | solution.py:34
  178.8 0.0 slice-done
  178.9 0.0 slice-done.1
  178.9 0.0 slice-done.2
  178.9 4.6 %convolution_convert_fusion = bf16[128,5120]{1,0:T(8,128)(2,1)} fusion(bf16[128,1024]{1,0:T(8,128)(2,1)S(1)} %bitcast.19, bf16[5120,1024]{1,0:T(8,128)(2,1)S(1)} %bitcast.17), kind=kOutput, calls=%fused_computation.3 | convolution fusion | flops 1342832640 | bytes 12058624 | tf_op jit(solution)/shard_map/dot_general | solution.py:35
  183.5 0.0 reduce-scatter.2.cloned.1.call-update
  183.5 39.5 %psum.7 = f32[8192]{0:T(1024)} all-reduce(f32[8192]{0:T(1024)S(1)} %get-tuple-element.2), channel_id=1, replica_groups=mesh['grp'=2,'dp'=4,'sp'=4] {'grp','dp','sp'}, use_global_device_ids=true, to_apply=%region_6.7 | all-reduce | flops 8192 | bytes 65536 | tf_op jit(solution)/shard_map/psum | solution.py:41
  (10 shorter events, 0.1 us)
Async XLA Ops:
  7.2 28.6 %all-gather.3.cloned.1.call-start = ((), (), s32[]{:S(2)}) async-start(), calls=%async_computation.3 | async-start | bytes 1474560 | tf_op jit(solution)/shard_map/all_gather | solution.py:10
  7.9 134.2 %all-gather.5.cloned.1.call-start = ((), (), s32[]{:S(2)}) async-start(), calls=%async_computation.4 | async-start | bytes 13107200 | tf_op jit(solution)/shard_map/all_gather | solution.py:11
  8.6 144.8 %copy-start.4 = (s32[8]{0:T(128)S(1)}, s32[8]{0:T(128)}, u32[]{:S(2)}) copy-start(s32[8]{0:T(128)} %param.9) | copy-start | bytes 100
  8.7 146.1 %copy-start.3 = (s32[16]{0:T(128)S(1)}, s32[16]{0:T(128)}, u32[]{:S(2)}) copy-start(s32[16]{0:T(128)} %param.10) | copy-start | bytes 196
  8.7 154.1 %copy-start = (bf16[128,8192]{1,0:T(8,128)(2,1)S(1)}, bf16[128,8192]{1,0:T(8,128)(2,1)}, u32[]{:S(2)}) copy-start(bf16[128,8192]{1,0:T(8,128)(2,1)} %param.11) | copy-start | bytes 6291460
  148.7 15.1 %copy-start.2 = (f32[8192]{0:T(1024)S(1)}, f32[8192]{0:T(1024)}, u32[]{:S(2)}) copy-start(f32[8192]{0:T(1024)} %param.13) | copy-start | bytes 98308
  148.7 14.1 %all-to-all-start = ((bf16[8,16,1024]{2,1,0:T(8,128)(2,1)}), bf16[8,16,1024]{2,1,0:T(8,128)(2,1)S(1)}, u32[]{:S(2)}, u32[]{:S(2)}) async-start(bf16[8,16,1024]{2,1,0:T(8,128)(2,1)} %bitcast), calls=%async_computation | async-start | bytes 524288 | tf_op jit(solution)/shard_map/all_to_all | solution.py:13
  153.4 69.6 %reduce-scatter.2.cloned.1.call-start = ((), (), s32[]{:S(2)}) async-start(), calls=%async_computation.5 | async-start | bytes 1474560 | tf_op jit(solution)/shard_map/reduce_scatter | solution.py:38
  162.8 1.6 copy-start.1
  162.8 16.0 %slice-start = ((s8[10485760]{0:T(1024)(128)(4,1)}), s8[4194304]{0:T(1024)(128)(4,1)S(1)}, s32[]{:S(2)}) async-start(s8[10485760]{0:T(1024)(128)(4,1)} %bitcast.16), calls=%async_computation.6 | async-start | bytes 8388608
  164.4 14.5 %slice-start.1 = ((s8[10485760]{0:T(1024)(128)(4,1)}), s8[4194304]{0:T(1024)(128)(4,1)S(1)}, s32[]{:S(2)}) async-start(s8[10485760]{0:T(1024)(128)(4,1)} %bitcast.16), calls=%async_computation.7 | async-start | bytes 8388608
  165.9 13.0 %slice-start.2 = ((s8[10485760]{0:T(1024)(128)(4,1)}), s8[2097152]{0:T(1024)(128)(4,1)S(1)}, s32[]{:S(2)}) async-start(s8[10485760]{0:T(1024)(128)(4,1)} %bitcast.16), calls=%async_computation.8 | async-start | bytes 4194304
Sparse Core Ops, SparseCore 0:
  9.6 26.1 all-gather.2
  37.6 104.4 all-gather.4
  183.6 34.8 reduce-scatter.1
where the time goes:
time: 230 us
  waiting for transfers between devices  143 us (62%)
  blocking collectives  51.3 us (22%)
  between operations  13.9 us (6%)
  matrix products  13.4 us (6%)
  starting transfers between devices  4.85 us (2%)
  other arithmetic  2.91 us (1%)
    all_gather x1, waiting for transfers between devices, body(): full_weight = lax.all_gather(merge_weight, 'dp', axis=0, tiled=True)  106 us
    psum x1, blocking collectives, body(): gain_grad = lax.psum(part_gain, ('grp', 'dp', 'sp'))  39.5 us
    all_gather x1, waiting for transfers between devices, body(): group_vis = lax.all_gather(vis, ('grp', 'sp'), axis=0, tiled=True)  27.1 us
    all_to_all x1, blocking collectives, body(): lax.all_to_all(demb, ('grp', 'sp'), split_axis=1, concat_axis=0, tiled=True)  11.8 us
    all_to_all x1, waiting for transfers between devices, body(): lax.all_to_all(partial_value.astype(jnp.bfloat16), ('grp', 'sp'), split_a...  7.9 us
    dot_general x1, matrix products, body(): jnp.dot(group_vis, full_weight, preferred_element_type=jnp.float32)  6.62 us
    all_to_all x1, starting transfers between devices, body(): lax.all_to_all(partial_value.astype(jnp.bfloat16), ('grp', 'sp'), split_a...  4.74 us
    dot_general x1, matrix products, body(): lax.dot_general(returned, full_weight, (((1,), (1,)), ((), ())), preferre...  4.62 us
  transfers between devices with their start and end apart: 4, of which 3 were waited for; matrix products, arithmetic and copies ran while one was open for 1% of the time, Pallas kernels for 0%

commit v1 on v0

--- a/solution.py
+++ b/solution.py
@@ -38,7 +38,8 @@
     vis_grad = lax.psum_scatter(
         terms.astype(jnp.bfloat16), ("grp", "sp"), scatter_dimension=0, tiled=True
     )
-    gain_grad = lax.psum(part_gain, ("grp", "dp", "sp"))
+    block_out = lax.all_gather(part_gain, axis_name=("grp", "dp", "sp"))
+    gain_grad = jnp.sum(block_out, 0)
     return (vis_grad, gain_grad)
 
 

time: 230 us -> 267 us (1.16)
  waiting for transfers between devices: 143 us -> 208 us
  blocking collectives: 51.3 us -> 12.2 us
  matrix products: 13.4 us -> 19.5 us
  local copies, waits for them, and re-layouts: 0.62 us -> 3.59 us
    psum x1 -> x0, blocking collectives: 39.5 us -> none  [body(): gain_grad = lax.psum(part_gain, ('grp', 'dp', 'sp'))]
    reduce_scatter x1, waiting for transfers between devices: 0.01 us -> 36.9 us  [body(): lax.psum_scatter(terms.astype(jnp.bfloat16), ('grp', 'sp'), scatter_dimen...]
    all_gather x0 -> x1, waiting for transfers between devices: none -> 28.4 us  [body(): block_out = lax.all_gather(part_gain, axis_name=('grp', 'dp', 'sp'))]
    dot_general x1, matrix products: 4.62 us -> 8.63 us  [body(): lax.dot_general(returned, full_weight, (((1,), (1,)), ((), ())), preferre...]
  transfers between devices with their start and end apart: 4 -> 5, of which waited for: 3 -> 5; matrix products, arithmetic and copies ran while one was open for 1% -> 6% of each run, Pallas kernels for 0% -> 0%
where the time goes in v1:
time: 267 us; the launch traced here: 266 us
  waiting for transfers between devices  208 us (78%)
  matrix products  19.5 us (7%)
  between operations  13.9 us (5%)
  blocking collectives  12.2 us (5%)
  starting transfers between devices  4.89 us (2%)
  other arithmetic  4.12 us (2%)
  local copies, waits for them, and re-layouts  3.59 us (1%)
    all_gather x1, waiting for transfers between devices, body(): full_weight = lax.all_gather(merge_weight, 'dp', axis=0, tiled=True)  106 us
    reduce_scatter x1, waiting for transfers between devices, body(): lax.psum_scatter(terms.astype(jnp.bfloat16), ('grp', 'sp'), scatter_dimen...  36.9 us
    all_gather x1, waiting for transfers between devices, body(): block_out = lax.all_gather(part_gain, axis_name=('grp', 'dp', 'sp'))  28.4 us
    all_gather x1, waiting for transfers between devices, body(): group_vis = lax.all_gather(vis, ('grp', 'sp'), axis=0, tiled=True)  27.1 us
    all_to_all x1, blocking collectives, body(): lax.all_to_all(demb, ('grp', 'sp'), split_axis=1, concat_axis=0, tiled=True)  12.2 us
    dot_general x1, matrix products, body(): lax.dot_general(returned, full_weight, (((1,), (1,)), ((), ())), preferre...  8.63 us
    all_to_all x1, waiting for transfers between devices, body(): lax.all_to_all(partial_value.astype(jnp.bfloat16), ('grp', 'sp'), split_a...  7.9 us
    dot_general x1, matrix products, body(): jnp.dot(group_vis, full_weight, preferred_element_type=jnp.float32)  6.62 us
  transfers between devices with their start and end apart: 5, of which 5 were waited for; matrix products, arithmetic and copies ran while one was open for 6% of the time, Pallas kernels for 0%

profile of v1, /device:TPU:0, one launch (start us, length us, event | category | flops | bytes accessed | tf_op | source)
XLA Modules:
  0.0 266.1 jit_solution(14880978807388212725)
XLA Ops:
  7.2 0.0 all-gather.5.cloned.1.call-start
  7.2 0.7 all-gather.5.cloned.1.call-update
  7.9 0.0 all-gather.7.cloned.1.call-start
  7.9 0.7 all-gather.7.cloned.1.call-update
  8.6 0.0 copy-start.6
  8.7 0.0 copy-start.5
  8.7 0.0 copy-start.1
  8.7 27.1 %all-gather.5.cloned.1.call-done = bf16[128,5120]{1,0:T(8,128)(2,1)} async-done(((bf16[16,5120]{1,0:T(8,128)(2,1)}), bf16[128,5120]{1,0:T(8,128)(2,1)}) %all-gather.5.cloned.1.call-update) | async-done | bytes 1310736 | tf_op jit(solution)/shard_map/all_gather | solution.py:10
  35.7 106.3 %all-gather.7.cloned.1.call-done = bf16[5120,1024]{1,0:T(8,128)(2,1)} async-done(((bf16[1280,1024]{1,0:T(8,128)(2,1)}), bf16[5120,1024]{1,0:T(8,128)(2,1)}) %all-gather.7.cloned.1.call-update) | async-done | bytes 10485776 | tf_op jit(solution)/shard_map/all_gather | solution.py:11
  142.1 6.6 %convolution_convert_fusion.1 = bf16[128,1024]{1,0:T(8,128)(2,1)} fusion(bf16[128,5120]{1,0:T(8,128)(2,1)} %all-gather.5.cloned.1.call-done, bf16[5120,1024]{1,0:T(8,128)(2,1)} %all-gather.7.cloned.1.call-done), kind=kOutput, calls=%fused_computation.14 | convolution fusion | flops 1342308352 | bytes 12058624 | tf_op jit(solution)/shard_map/dot_general | solution.py:12
  148.7 4.7 %all-to-all-start = ((bf16[8,16,1024]{2,1,0:T(8,128)(2,1)}), bf16[8,16,1024]{2,1,0:T(8,128)(2,1)S(1)}, u32[]{:S(2)}, u32[]{:S(2)}) async-start(bf16[8,16,1024]{2,1,0:T(8,128)(2,1)} %bitcast), calls=%async_computation | async-start | bytes 524288 | tf_op jit(solution)/shard_map/all_to_all | solution.py:13
  153.4 0.0 all-gather.9.cloned.1.call-start
  153.5 0.0 copy-done.6
  153.5 0.6 reduce_sum.45
  154.1 0.7 add_compare_fusion
  154.8 0.1 fusion.12
  154.9 7.9 %all-to-all-done = bf16[8,16,1024]{2,1,0:T(8,128)(2,1)S(1)} async-done(((bf16[8,16,1024]{2,1,0:T(8,128)(2,1)}), bf16[8,16,1024]{2,1,0:T(8,128)(2,1)S(1)}, u32[]{:S(2)}, u32[]{:S(2)}) %all-to-all-start) | async-done | bytes 262176 | tf_op jit(solution)/shard_map/all_to_all | solution.py:13
  162.8 0.0 copy-done.1
  162.8 1.0 multiply_reduce_fusion
  163.8 0.0 copy-start.3
  163.8 2.1 copy-done
  165.9 2.0 fusion.7
  168.0 0.0 all-gather.9.cloned.1.call-update
  168.0 0.0 reduce-scatter.2.cloned.1.call-start
  168.1 3.3 %fusion = bf16[16,8192]{1,0:T(8,128)(2,1)S(1)} fusion(bf16[128,8192]{1,0:T(8,128)(2,1)S(1)} %copy-done.3, f32[128,8192]{1,0:T(8,128)} %copy-done, f32[128]{0:T(128)S(1)} %broadcast_multiply_fusion, f32[128]{0:T(128)S(1)} %get-tuple-element.4, f32[8192]{0:T(1024)S(1)} %copy-done.4, f32[128]{0:T(128)S(1)} %get-tuple-element.5, ...), kind=kOutput, calls=%fused_computation.2 | convolution fusion | flops 41160704 | bytes 6587984 | tf_op jit(solution)/shard_map/dot_general | solution.py:32
  171.3 12.2 %all_to_all.38 = bf16[16,8,1024]{2,0,1:T(8,128)(2,1)S(1)} all-to-all(bf16[16,8,1024]{2,0,1:T(8,128)(2,1)S(1)} %bitcast.19), channel_id=1, replica_groups=mesh['grp'=2,'dp'=4,'sp'=4] {'grp','sp'}, dimensions={1} | all-to-all | bytes 524288 | tf_op jit(solution)/shard_map/all_to_all | solution.py:34
  183.5 8.6 %convolution_convert_fusion = bf16[128,5120]{1,0:T(8,128)(2,1)} fusion(bf16[128,1024]{1,0:T(8,128)(2,1)S(1)} %bitcast.17, bf16[5120,1024]{1,0:T(8,128)(2,1)} %all-gather.7.cloned.1.call-done), kind=kOutput, calls=%fused_computation.3 | convolution fusion | flops 1342832640 | bytes 12058624 | tf_op jit(solution)/shard_map/dot_general | solution.py:35
  192.2 0.0 reduce-scatter.2.cloned.1.call-update
  192.2 28.4 %all-gather.9.cloned.1.call-done = f32[262144]{0:T(1024)} async-done(((f32[8192]{0:T(1024)}), f32[262144]{0:T(1024)}) %all-gather.9.cloned.1.call-update) | async-done | bytes 1048592 | tf_op jit(solution)/shard_map/all_gather | solution.py:41
  220.6 1.4 reshape.41
  222.0 0.7 reduce_sum.49
  222.7 36.9 %reduce-scatter.2.cloned.1.call-done = bf16[16,5120]{1,0:T(8,128)(2,1)} async-done(((bf16[128,5120]{1,0:T(8,128)(2,1)}), bf16[16,5120]{1,0:T(8,128)(2,1)}) %reduce-scatter.2.cloned.1.call-update) | async-done | bytes 163856 | tf_op jit(solution)/shard_map/reduce_scatter | solution.py:38
  (11 shorter events, 0.1 us)
Async XLA Ops:
  7.2 28.6 %all-gather.5.cloned.1.call-start = ((), (), s32[]{:S(2)}) async-start(), calls=%async_computation.3 | async-start | bytes 1474560 | tf_op jit(solution)/shard_map/all_gather | solution.py:10
  7.9 134.2 %all-gather.7.cloned.1.call-start = ((), (), s32[]{:S(2)}) async-start(), calls=%async_computation.4 | async-start | bytes 13107200 | tf_op jit(solution)/shard_map/all_gather | solution.py:11
  8.6 144.8 %copy-start.6 = (s32[8]{0:T(128)S(1)}, s32[8]{0:T(128)}, u32[]{:S(2)}) copy-start(s32[8]{0:T(128)} %param.9) | copy-start | bytes 100
  8.7 146.1 %copy-start.5 = (s32[16]{0:T(128)S(1)}, s32[16]{0:T(128)}, u32[]{:S(2)}) copy-start(s32[16]{0:T(128)} %param.10) | copy-start | bytes 196
  8.7 154.1 %copy-start.1 = (bf16[128,8192]{1,0:T(8,128)(2,1)S(1)}, bf16[128,8192]{1,0:T(8,128)(2,1)}, u32[]{:S(2)}) copy-start(bf16[128,8192]{1,0:T(8,128)(2,1)} %param.11) | copy-start | bytes 6291460
  148.7 17.2 %copy-start.4 = (f32[8192]{0:T(1024)S(1)}, f32[8192]{0:T(1024)}, u32[]{:S(2)}) copy-start(f32[8192]{0:T(1024)} %param.13) | copy-start | bytes 98308
  148.7 14.1 %all-to-all-start = ((bf16[8,16,1024]{2,1,0:T(8,128)(2,1)}), bf16[8,16,1024]{2,1,0:T(8,128)(2,1)S(1)}, u32[]{:S(2)}, u32[]{:S(2)}) async-start(bf16[8,16,1024]{2,1,0:T(8,128)(2,1)} %bitcast), calls=%async_computation | async-start | bytes 524288 | tf_op jit(solution)/shard_map/all_to_all | solution.py:13
  153.4 67.1 %all-gather.9.cloned.1.call-start = ((), (), s32[]{:S(2)}) async-start(), calls=%async_computation.6 | async-start | bytes 1081344 | tf_op jit(solution)/shard_map/all_gather | solution.py:41
  162.8 3.1 %copy-start.2 = (bf16[128,8192]{1,0:T(8,128)(2,1)S(1)}, bf16[128,8192]{1,0:T(8,128)(2,1)}, u32[]{:S(2)}) copy-start(bf16[128,8192]{1,0:T(8,128)(2,1)} %param.12) | copy-start | bytes 6291460
  163.8 2.1 copy-start
  163.8 4.3 %copy-start.3 = (bf16[128,8192]{1,0:T(8,128)(2,1)S(1)}, bf16[128,8192]{1,0:T(8,128)(2,1)}, u32[]{:S(2)}) copy-start(bf16[128,8192]{1,0:T(8,128)(2,1)} %param.12) | copy-start | bytes 6291460
  168.0 91.6 %reduce-scatter.2.cloned.1.call-start = ((), (), s32[]{:S(2)}) async-start(), calls=%async_computation.5 | async-start | bytes 1474560 | tf_op jit(solution)/shard_map/reduce_scatter | solution.py:38
Sparse Core Ops, SparseCore 0:
  9.6 26.1 all-gather.4
  37.6 104.4 all-gather.6
  168.1 52.4 all-gather.8
  223.3 36.2 reduce-scatter.1
